TPU v7x, 32 devices: a whole 2x2x4 slice. The times are simulated.
32 devices in a mesh: tile: 4 (over z), chan: 4 (over y, x), tm: 2 (over core).
Axes of the slice: x: 2, y: 2, z: 4, core: 2. Of those that a mesh axis runs over, the one named last changes fastest.
Arguments:
- observed_values: bfloat16 [2, 65536, 128], P('tm', ('tile', 'chan')), may hold values from -6 to 6
- observed_tile: int32 [2, 65536, 1], P('tm', ('tile', 'chan')), may hold values from 0 to 3; in each aligned block of 4096 rows (0 to 4095, 4096 to 8191, ..., all dimensions but the last counted through in order) at most 2048 rows name the same one
- observed_cell: int32 [2, 65536], P('tm', ('tile', 'chan')), may hold values from 0 to 2047
- patch_weight: bfloat16 [4, 256, 256], P(None, None, 'chan'), may hold values from -0.1875 to 0.1875
- depth_weight: bfloat16 [9, 256], P(None, 'chan'), may hold values from -2 to 2
- owners: int32 [4, 4], replicated, may hold values from 0 to 3, as said below
Outputs:
- owned: bfloat16 [4, 2, 4, 64, 256], P('tile', 'tm', None, None, 'chan')
Inputs may be any that keep to these rules, and one draw needn't show every extreme that they name: `observed_tile`: in the rows of one device at most 2048 name the same tile. owners[t, j] - t is the same modulo 4 for every t and differs between any two j, so every row and every column of owners is a permutation.
All inputs are finite; a program needn't handle non-finite values.
Results may differ from a plain program's by a relative error of at most 0.014.
Values may be sent and summed in bfloat16 or wider, within the bound.
A program may use at most 64 MiB of HBM per device.

v0:
```python
import jax
import jax.numpy as jnp
from jax import lax
from jax.sharding import PartitionSpec as P

V = 128
HS = 32
WS = 64


def padded(x, sides, width):
    for axis, dim in sides:
        devices, length = (lax.axis_size(axis), x.shape[dim])
        up = [(i, (i + 1) % devices) for i in range(devices - 1)]
        down = [(j, i) for i, j in up]
        last = lax.slice_in_dim(x, length - width, length, axis=dim)
        first = lax.slice_in_dim(x, 0, width, axis=dim)
        before = lax.ppermute(last, axis, up)
        after = lax.ppermute(first, axis, down)
        x = jnp.concatenate([before, x, after], axis=dim)
    return x


def pack_rows(values, destination, placed, tile_count, capacity):
    match = (destination[:, None] == lax.iota(jnp.int32, tile_count)[None, :]).astype(jnp.int32)
    earlier = jnp.cumsum(match, axis=0) - match
    position = jnp.sum(earlier * match, axis=1)
    slot_index = destination * capacity + position
    width = values.shape[1]
    sent_values = jnp.zeros((tile_count * capacity, width), jnp.bfloat16).at[slot_index].set(values)
    sent_cells = jnp.full((tile_count * capacity,), -1, jnp.int32).at[slot_index].set(placed)
    return (
        sent_values.reshape(tile_count, capacity, width),
        sent_cells.reshape(tile_count, capacity),
    )


def grid_block(arrived_values, arrived_cells, first_cell):
    cell_ids = first_cell + lax.iota(jnp.int32, 128)
    matches = cell_ids[:, None] == arrived_cells[None, :]
    totals = jnp.dot(
        matches.astype(jnp.bfloat16), arrived_values, preferred_element_type=jnp.float32
    )
    counts = jnp.sum(matches.astype(jnp.float32), axis=1)
    return (totals, counts)


def patch_rows(field, weight, row_start, row_count):
    slab = lax.dynamic_slice_in_dim(field, 2 * row_start, 2 * row_count, 0)
    depth_in = field.shape[2]
    result = jnp.zeros((row_count * (field.shape[1] // 2), weight.shape[2]), jnp.float32)
    for tap_row in range(2):
        for tap_col in range(2):
            window = slab[tap_row::2, tap_col::2, :].reshape(-1, depth_in)
            result = result + jnp.dot(
                window, weight[tap_row * 2 + tap_col], preferred_element_type=jnp.float32
            )
    return result.reshape(row_count, field.shape[1] // 2, weight.shape[2])


def local(observed_values, observed_tile, observed_cell, patch_weight, depth_weight, owners):
    tile_count = lax.axis_size("tile")
    slot_count = lax.axis_size("tm")
    values = observed_values[0]
    capacity = 2 * values.shape[0] // tile_count
    sent_values, sent_cells = pack_rows(
        values, observed_tile[0, :, 0], observed_cell[0], tile_count, capacity
    )
    arrived = (
        lax.all_to_all(sent_values, "tile", split_axis=0, concat_axis=0, tiled=True),
        lax.all_to_all(sent_cells, "tile", split_axis=0, concat_axis=0, tiled=True),
    )
    arrived_values = arrived[0].reshape(-1, V)
    arrived_cells = arrived[1].reshape(-1)
    cell_count = HS * WS
    firsts = jnp.arange(cell_count // 128, dtype=jnp.int32) * 128
    totals, counts = lax.map(
        lambda first_cell: grid_block(arrived_values, arrived_cells, first_cell), firsts
    )
    totals = totals.reshape(cell_count, V)
    counts = counts.reshape(cell_count)
    totals, counts = (
        lax.psum(totals.astype(jnp.bfloat16), "chan").astype(jnp.float32),
        lax.psum(counts.astype(jnp.bfloat16), "chan").astype(jnp.float32),
    )
    means = (totals / jnp.maximum(counts, 1.0)[:, None]).astype(jnp.bfloat16)
    means = means.reshape(HS, WS, V)
    out_rows = HS // (2 * slot_count)
    half_cols = WS // 2
    stacked = lax.all_gather(means, "tm", axis=2, tiled=True)
    encoded = patch_rows(stacked, patch_weight, lax.axis_index("tm") * out_rows, out_rows)
    hidden = jax.nn.gelu(encoded).astype(jnp.bfloat16)
    rimmed = padded(hidden, ((("tile", "tm"), 0),), 2)
    widened = jnp.pad(rimmed, ((0, 0), (2, 2), (0, 0))).astype(jnp.float32)
    depth = jnp.zeros(hidden.shape, jnp.float32)
    for tap_row in range(3):
        for tap_col in range(3):
            shifted = widened[
                2 * tap_row : 2 * tap_row + out_rows, 2 * tap_col : 2 * tap_col + half_cols, :
            ]
            depth = depth + shifted * depth_weight[tap_row * 3 + tap_col].astype(jnp.float32)
    latent = (hidden.astype(jnp.float32) + depth).astype(jnp.bfloat16)
    channels = latent.shape[2]
    pieces = latent.reshape(tile_count, -1, channels)
    own_row = lax.dynamic_index_in_dim(owners, lax.axis_index("tile"), 0, keepdims=False)
    order = lax.iota(jnp.int32, tile_count)
    chosen = jnp.sum(
        order[None, :] * (own_row[None, :] == order[:, None]).astype(jnp.int32), axis=1
    )
    outgoing = pieces[chosen]
    received = lax.all_to_all(outgoing, "tile", split_axis=0, concat_axis=0, tiled=True)
    return received.reshape(1, 1, tile_count, -1, channels)


def solution(mesh):
    placed = (
        P("tm", ("tile", "chan"), None),
        P("tm", ("tile", "chan"), None),
        P("tm", ("tile", "chan")),
        P(None, None, "chan"),
        P(None, "chan"),
        P(),
    )
    return jax.shard_map(
        local,
        mesh=mesh,
        in_specs=placed,
        out_specs=P("tile", "tm", None, None, "chan"),
        check_vma=False,
    )
```

profile of v0, /device:TPU:0, one launch (start us, length us, event | category | flops | bytes accessed | tf_op | source)
XLA Modules:
  0.0 239.9 jit_solution(12376599636071230112)
XLA Ops:
  7.3 1.1 reduce-window.6
  10.6 16.3 %scatter_custom_fusion = s32[8192]{0:T(1024)} fusion(s32[4096]{0:T(1024)S(1)} %bitcast.137, s32[4096]{0:T(1024)} %bitcast.141, s32[]{:T(128)} %constant.27.clone.1), kind=kCustom, calls=%fused_computation.77 | custom fusion | bytes 33280 | tf_op jit(solution)/shard_map/scatter | solution.py:31
  26.9 6.3 %all-to-all-start = ((s32[4,1,2048]{2,1,0:T(1,128)}), s32[4,1,2048]{2,1,0:T(1,128)S(1)}, u32[]{:S(2)}, u32[]{:S(2)}) async-start(s32[4,1,2048]{2,1,0:T(1,128)} %bitcast.10), calls=%async_computation | async-start | bytes 65536 | tf_op jit(solution)/shard_map/all_to_all | solution.py:71
  33.2 12.4 %scatter_custom_fusion.1 = bf16[8192,128]{1,0:T(8,128)(2,1)} fusion(s32[4096]{0:T(1024)S(1)} %bitcast.138, bf16[1,4096,128]{2,1,0:T(8,128)(2,1)S(1)} %copy-done, bf16[]{:T(256)} %constant.19.clone.1), kind=kCustom, calls=%fused_computation.15 | custom fusion | bytes 3145730 | tf_op jit(solution)/shard_map/scatter | solution.py:30
  45.6 5.1 %all-to-all-start.1 = ((bf16[4,2048,128]{2,1,0:T(8,128)(2,1)}), bf16[4,2048,128]{2,1,0:T(8,128)(2,1)S(1)}, u32[]{:S(2)}, u32[]{:S(2)}) async-start(bf16[4,2048,128]{2,1,0:T(8,128)(2,1)} %bitcast.12), calls=%async_computation.1 | async-start | bytes 4194304 | tf_op jit(solution)/shard_map/all_to_all | solution.py:70
  50.8 47.6 %all-to-all-done.1 = bf16[4,2048,128]{2,1,0:T(8,128)(2,1)S(1)} async-done(((bf16[4,2048,128]{2,1,0:T(8,128)(2,1)}), bf16[4,2048,128]{2,1,0:T(8,128)(2,1)S(1)}, u32[]{:S(2)}, u32[]{:S(2)}) %all-to-all-start.1) | async-done | bytes 2097184 | tf_op jit(solution)/shard_map/all_to_all | solution.py:70
  98.4 56.3 %while.12 = (s32[]{:T(128)}, bf16[16,128,128]{2,1,0:T(8,128)(2,1)}, bf16[16,128]{1,0:T(8,128)(2,1)S(1)}, s32[16]{0:T(128)S(1)}, s32[4,2048]{1,0:T(4,128)S(1)}, /...) while((s32[]{:T(128)}, bf16[16,128,128]{2,1,0:T(8,128)(2,1)}, bf16[16,128]{1,0:T(8,128)(2,1)S(1)}, ...), condition=%wide.region_7.8_spmd, body=%wide.region_5.7_spmd.sunk | while | flops 272629760 | bytes 2296681 | solution.py:77
  99.7 1.5 fusion.67
  103.3 1.5 fusion.67
  106.8 1.5 fusion.67
  110.3 1.5 fusion.67
  113.8 1.5 fusion.67
  117.3 1.5 fusion.67
  120.9 1.5 fusion.67
  124.4 1.5 fusion.67
  127.9 1.5 fusion.67
  131.4 1.5 fusion.67
  134.9 1.5 fusion.67
  138.5 1.5 fusion.67
  142.0 1.5 fusion.67
  145.5 1.5 fusion.67
  149.0 1.5 fusion.67
  152.5 1.5 fusion.67
  154.8 10.1 %psum.15 = bf16[2048]{0:T(1024)(128)(2,1)S(1)} all-reduce(bf16[2048]{0:T(1024)(128)(2,1)S(1)} %bitcast.140), channel_id=1, replica_groups=mesh['tile'=4,'chan'=4,'tm'=2] {'chan'}, use_global_device_ids=true, to_apply=%region_9.10 | all-reduce | flops 2048 | bytes 8192 | tf_op jit(solution)/shard_map/psum | solution.py:84
  164.9 34.5 %all-reduce.3.cloned.1.call-done = bf16[2048,128]{1,0:T(8,128)(2,1)} async-done(((bf16[2048,128]{1,0:T(8,128)(2,1)}), bf16[2048,128]{1,0:T(8,128)(2,1)}) %all-reduce.3.cloned.1.call-update) | async-done | bytes 524304 | tf_op jit(solution)/shard_map/psum | solution.py:83
  199.4 2.2 divide_convert_fusion
  202.5 8.1 %all-gather.2.cloned.1.call-done = bf16[32,64,256]{2,1,0:T(8,128)(2,1)} async-done(((bf16[32,64,128]{2,1,0:T(8,128)(2,1)}), bf16[32,64,256]{2,1,0:T(8,128)(2,1)}) %all-gather.2.cloned.1.call-update) | async-done | bytes 1048592 | tf_op jit(solution)/shard_map/all_gather | solution.py:90
  210.6 1.1 constant_dynamic-slice_fusion
  214.1 2.2 collective-permute-start
  216.2 1.3 collective-permute-start.1
  217.6 2.9 %collective-permute-done.1 = bf16[2,32,64]{2,1,0:T(8,128)(2,1)S(1)} collective-permute-done((bf16[2,32,64]{2,1,0:T(8,128)(2,1)S(1)}, bf16[2,32,64]{2,1,0:T(8,128)(2,1)S(1)}, u32[]{:S(2)}, u32[]{:S(2)}) %collective-permute-start.1) | collective-permute-done | bytes 8224 | tf_op jit(solution)/shard_map/ppermute | solution.py:19
  221.4 11.0 %all_to_all.22 = bf16[4,2,2048]{2,1,0:T(2,128)(2,1)S(1)} all-to-all(bf16[4,2,2048]{2,1,0:T(2,128)(2,1)S(1)} %reshape.214), channel_id=1, replica_groups=mesh['tile'=4,'chan'=4,'tm'=2] {'tile'}, dimensions={0} | all-to-all | bytes 65536 | tf_op jit(solution)/shard_map/all_to_all | solution.py:111
  (124 shorter events, 40.1 us)
Async XLA Ops:
  6.5 26.7 %copy-start = (bf16[1,4096,128]{2,1,0:T(8,128)(2,1)S(1)}, bf16[1,4096,128]{2,1,0:T(8,128)(2,1)}, u32[]{:S(2)}) copy-start(bf16[1,4096,128]{2,1,0:T(8,128)(2,1)} %param.8) | copy-start | bytes 3145732
  26.9 18.8 %all-to-all-start = ((s32[4,1,2048]{2,1,0:T(1,128)}), s32[4,1,2048]{2,1,0:T(1,128)S(1)}, u32[]{:S(2)}, u32[]{:S(2)}) async-start(s32[4,1,2048]{2,1,0:T(1,128)} %bitcast.10), calls=%async_computation | async-start | bytes 65536 | tf_op jit(solution)/shard_map/all_to_all | solution.py:71
  45.6 52.7 %all-to-all-start.1 = ((bf16[4,2048,128]{2,1,0:T(8,128)(2,1)}), bf16[4,2048,128]{2,1,0:T(8,128)(2,1)S(1)}, u32[]{:S(2)}, u32[]{:S(2)}) async-start(bf16[4,2048,128]{2,1,0:T(8,128)(2,1)} %bitcast.12), calls=%async_computation.1 | async-start | bytes 4194304 | tf_op jit(solution)/shard_map/all_to_all | solution.py:70
  50.7 148.7 %all-reduce.3.cloned.1.call-start = ((), (), s32[]{:S(2)}) async-start(), calls=%async_computation.3 | async-start | bytes 1048576 | tf_op jit(solution)/shard_map/psum | solution.py:83
  154.7 47.8 %copy-start.2 = (bf16[9,64]{1,0:T(8,128)(2,1)S(1)}, bf16[9,64]{1,0:T(8,128)(2,1)}, u32[]{:S(2)}) copy-start(bf16[9,64]{1,0:T(8,128)(2,1)} %param.12) | copy-start | bytes 3460
  154.7 58.4 %copy-start.1 = (bf16[4,256,64]{1,2,0:T(8,128)(2,1)S(1)}, bf16[4,256,64]{1,2,0:T(8,128)(2,1)}, u32[]{:S(2)}) copy-start(bf16[4,256,64]{1,2,0:T(8,128)(2,1)} %param.11) | copy-start | bytes 393220
  154.7 55.8 %all-gather.2.cloned.1.call-start = ((), (), s32[]{:S(2)}) async-start(), calls=%async_computation.4 | async-start | bytes 1572864 | tf_op jit(solution)/shard_map/all_gather | solution.py:90
  214.1 3.5 %collective-permute-start = (bf16[2,32,64]{2,1,0:T(8,128)(2,1)S(1)}, bf16[2,32,64]{2,1,0:T(8,128)(2,1)S(1)}, u32[]{:S(2)}, u32[]{:S(2)}) collective-permute-start(bf16[2,32,64]{2,1,0:T(8,128)(2,1)S(1)} %get-tuple-element.52), channel_id=1, source_target_pairs={{0,1},{1,8},{8,9},{9,16},{16,17},{17,24},{24,25},{2,3},{3,10},{10,... | collective-permute-start | bytes 24584 | tf_op jit(solution)/shard_map/ppermute | solution.py:18
  216.2 4.2 %collective-permute-start.1 = (bf16[2,32,64]{2,1,0:T(8,128)(2,1)S(1)}, bf16[2,32,64]{2,1,0:T(8,128)(2,1)S(1)}, u32[]{:S(2)}, u32[]{:S(2)}) collective-permute-start(bf16[2,32,64]{2,1,0:T(8,128)(2,1)S(1)} %get-tuple-element.53), channel_id=1, source_target_pairs={{1,0},{8,1},{9,8},{16,9},{17,16},{24,17},{25,24},{3,2},{10,3},{11,... | collective-permute-start | bytes 24584 | tf_op jit(solution)/shard_map/ppermute | solution.py:19
Sparse Core Ops, SparseCore 0:
  154.9 44.5 all-reduce.2
  201.8 8.7 all-gather.1
where the time goes:
time: 241 us; the launch traced here: 240 us
  waiting for transfers between devices  93.1 us (39%)
  local copies, waits for them, and re-layouts  45 us (19%)
  other arithmetic  27.5 us (11%)
  matrix products  24.4 us (10%)
  blocking collectives  21.1 us (9%)
  starting transfers between devices  14.9 us (6%)
  between operations  13.6 us (6%)
    all_to_all x1, waiting for transfers between devices, local(): lax.all_to_all(sent_values, 'tile', split_axis=0, concat_axis=0, tiled=True)  47.6 us
    psum x1, waiting for transfers between devices, local(): lax.psum(totals.astype(jnp.bfloat16), 'chan').astype(jnp.float32)  34.5 us
    dot_general x16, matrix products, grid_block(): jnp.dot(matches.astype(jnp.bfloat16), arrived_values, preferred_element_t...  23.7 us
    scatter x1, local copies, waits for them, and re-layouts, pack_rows(): jnp.full((tile_count * capacity,), -1, jnp.int32).at[slot_index].set(placed)  16.3 us
    scatter x1, local copies, waits for them, and re-layouts, pack_rows(): jnp.zeros((tile_count * capacity, width), jnp.bfloat16).at[slot_index]  12.4 us
    add x16, other arithmetic, grid_block(): cell_ids = first_cell + lax.iota(jnp.int32, 128)  11 us
    all_to_all x1, blocking collectives, local(): lax.all_to_all(outgoing, 'tile', split_axis=0, concat_axis=0, tiled=True)  11 us
    dynamic_slice x16, local copies, waits for them, and re-layouts, local(): lax.map(lambda first_cell: grid_block(arrived_values, arrived_cells, firs...  10.7 us
  transfers between devices with their start and end apart: 6, of which 4 were waited for; matrix products, arithmetic and copies ran while one was open for 6% of the time, Pallas kernels for 0%

commit v1 on v0

--- a/solution.py
+++ b/solution.py
@@ -1,6 +1,9 @@
+import functools
 import jax
 import jax.numpy as jnp
 from jax import lax
+from jax.experimental import pallas as pl
+from jax.experimental.pallas import tpu as pltpu
 from jax.sharding import PartitionSpec as P
 
 V = 128
@@ -112,6 +115,341 @@
     return received.reshape(1, 1, tile_count, -1, channels)
 
 
+def fused_kernel(
+    values_ref, tile_ref, cell_ref, weight_ref, depth_ref, owners_ref, out_ref,
+    masked, onehot, position, partial, first, second_src, second, third_src, third,
+    count_src, count_in, weights, mean_src, mean_in, means, hidden_src, hidden_all,
+    weight_send, weight_recv, pass_send, pass_recv, count_send, count_recv,
+    first_send, first_recv, second_send, second_recv, third_send, third_recv,
+    mean_send, mean_recv, hidden_send, hidden_recv,
+):
+    f32, bf16 = jnp.float32, jnp.bfloat16
+    n_tile, n_chan, n_core = (lax.axis_size(a) for a in ("tile", "chan", "tm"))
+    me_t, me_c, me_s = (lax.axis_index(a) for a in ("tile", "chan", "tm"))
+    rows, width = values_ref.shape
+    block = partial.shape[3]
+    quarter = block // 4
+    flip_x = me_c + 1 - 2 * (me_c % 2)
+    flip_y = (me_c + 2) % 4
+    diagonal = 3 - me_c
+    near = (flip_x, flip_y)
+    far = (flip_y, flip_x)
+    other = 1 - me_s
+
+    def remote(source, target, send, recv, device):
+        return pltpu.make_async_remote_copy(
+            src_ref=source, dst_ref=target, send_sem=send, recv_sem=recv,
+            device_id=device, device_id_type=pl.DeviceIdType.MESH,
+        )
+
+    offsets = [
+        (a, b, c) for a in range(n_tile) for b in range(n_chan) for c in range(n_core)
+    ][1:]
+
+    def at(a, b, c):
+        return ((me_t + a) % n_tile, (me_c + b) % n_chan, (me_s + c) % n_core)
+
+    barrier = pltpu.get_barrier_semaphore()
+    for offset in offsets:
+        pl.semaphore_signal(
+            barrier, inc=1, device_id=at(*offset), device_id_type=pl.DeviceIdType.MESH
+        )
+
+    cell = cell_ref[...]
+    row, col = cell // WS, cell % WS
+    half_cols = WS // 2
+    band = row // 4
+    position[...] = (
+        band * block + (row % 2) * (2 * quarter) + (col % 2) * quarter
+        + ((row % 4) // 2) * half_cols + col // 2
+    )
+    weights[me_c] = weight_ref[...]
+
+    def mask_rows(i, carry):
+        span = pl.ds(pl.multiple_of(i * 128, 128), 128)
+        tiles = jnp.broadcast_to(tile_ref[:, span].astype(f32), (128, 128))
+        tiles = jnp.transpose(tiles)
+        taken = values_ref[span, :].astype(f32)
+        for t in range(n_tile):
+            masked[span, t * width:(t + 1) * width] = jnp.where(
+                tiles == float(t), taken, 0.0
+            ).astype(bf16)
+        return carry
+
+    lax.fori_loop(0, rows // 128, mask_rows, 0)
+
+    pos = position[...]
+    inner = pos % block
+    half = pos // (block * n_chan)
+    piece = (pos // block) % n_chan
+    code = ((tile_ref[...] * n_chan + piece) * 8 + half * 2 + inner // 128)
+    code_ids = lax.broadcasted_iota(jnp.int32, (n_tile * n_chan * 8, rows), 0)
+    lane_ids = lax.broadcasted_iota(jnp.int32, (128, rows), 0)
+    counts = lax.dot_general(
+        (code_ids == code).astype(bf16), (lane_ids == inner % 128).astype(bf16),
+        (((1,), (1,)), ((), ())), preferred_element_type=f32,
+    )
+    count_src[...] = counts.reshape(n_tile * n_chan, 8, 128)
+
+    pl.semaphore_wait(barrier, len(offsets))
+
+    def weight_copy(o):
+        here = weights.at[me_c, me_s]
+        return remote(
+            here, here, weight_send.at[o - 1], weight_recv.at[o - 1],
+            (me_t, (me_c + o) % n_chan, me_s),
+        )
+
+    def pass_copy(o):
+        here = weights.at[(me_c - o + n_chan) % n_chan, me_s]
+        return remote(
+            here, here, pass_send.at[o - 1], pass_recv.at[o - 1], (me_t, me_c, other)
+        )
+
+    def count_copy(a, b):
+        i = a * n_chan + b
+        to = ((me_t + a) % n_tile, (me_c + b) % n_chan, me_s)
+        return remote(
+            count_src.at[to[0] * n_chan + to[1]], count_in.at[i],
+            count_send.at[i], count_recv.at[i], to,
+        )
+
+    def first_copy(h, k, o, to):
+        t = (me_t + o) % n_tile
+        return remote(
+            partial.at[h, k, t], first.at[h, k, t],
+            first_send.at[h, k, o], first_recv.at[h, k, o], (me_t, to, me_s),
+        )
+
+    def second_copy(h, o):
+        t = (me_t + o) % n_tile
+        return remote(
+            second_src.at[h, t], second.at[h, t],
+            second_send.at[h, o], second_recv.at[h, o], (me_t, far[h], me_s),
+        )
+
+    def third_copy(h, o):
+        t = (me_t + o) % n_tile
+        return remote(
+            third_src.at[h, o], third.at[h, o],
+            third_send.at[h, o], third_recv.at[h, o], (t, me_c, me_s),
+        )
+
+    turns = tuple(range(1, n_tile)) + (0,)
+    for o in range(1, n_chan):
+        weight_copy(o).start()
+    for a in range(n_tile):
+        for b in range(n_chan):
+            if a or b:
+                count_copy(a, b).start()
+
+    def grid_block(step, carry):
+        h, k = step % 2, step // 2
+        to = near[0] * (1 - h) + near[1] * h
+        away = near[1] * (1 - h) + near[0] * h
+        picks = (diagonal, to, away, me_c)
+        j = sum(p * (1 - jnp.minimum(jnp.abs(k - i), 1)) for i, p in enumerate(picks))
+        base = (h * n_chan + j) * block
+        ids = lax.broadcasted_iota(jnp.int32, (block, rows), 0)
+        onehot[...] = (ids == position[...] - base).astype(bf16)
+        sums = jnp.dot(onehot[...], masked[...], preferred_element_type=f32)
+        for t in range(n_tile):
+            partial[h, k, t] = sums[:, t * width:(t + 1) * width].astype(bf16)
+
+        @pl.when(k < 2)
+        def _():
+            for o in turns:
+                first_copy(h, k, o, to).start()
+
+        return carry
+
+    lax.fori_loop(0, 8, grid_block, 0)
+
+    for o in turns:
+        t = (me_t + o) % n_tile
+        for h in range(2):
+            first_copy(h, 0, o, near[h]).wait_recv()
+            second_src[h, t] = (
+                partial[h, 2, t].astype(f32) + first[h, 0, t].astype(f32)
+            ).astype(bf16)
+            second_copy(h, o).start()
+    for o in range(1, n_chan):
+        weight_copy(o).wait_recv()
+        pass_copy(o).start()
+    for o in turns:
+        t = (me_t + o) % n_tile
+        for h in range(2):
+            first_copy(h, 1, o, near[h]).wait_recv()
+            second_copy(h, o).wait_recv()
+            third_src[h, o] = (
+                partial[h, 3, t].astype(f32)
+                + first[h, 1, t].astype(f32)
+                + second[h, t].astype(f32)
+            ).astype(bf16)
+            if o:
+                third_copy(h, o).start()
+
+    total = count_src[me_t * n_chan + me_c]
+    for a in range(n_tile):
+        for b in range(n_chan):
+            if a or b:
+                count_copy(a, b).wait_recv()
+                total = total + count_in[a * n_chan + b]
+    divisor = jnp.maximum(total, 1.0)
+
+    for h in range(2):
+        for o in range(1, n_tile):
+            third_copy(h, o).wait_recv()
+        summed = third_src[h, 0].astype(f32)
+        for o in range(1, n_tile):
+            summed = summed + third[h, o].astype(f32)
+        for u in range(block // 128):
+            line = divisor[h * 2 + u:h * 2 + u + 1, :]
+            each = jnp.transpose(jnp.broadcast_to(line, (128, 128)))
+            means[h, u * 128:(u + 1) * 128] = (summed[u * 128:(u + 1) * 128] / each).astype(bf16)
+
+    mean_src[...] = means[other]
+    mean_copy = remote(mean_src, mean_in, mean_send, mean_recv, (me_t, me_c, other))
+    mean_copy.start()
+    for o in range(1, n_chan):
+        pass_copy(o).wait_recv()
+    mean_copy.wait_recv()
+    mine, theirs = means[me_s], mean_in[...]
+    even = me_s == 0
+    slots = (jnp.where(even, mine, theirs), jnp.where(even, theirs, mine))
+    lane = lax.broadcasted_iota(jnp.int32, (half_cols, 128), 1)
+    for c in range(n_chan):
+        taps = []
+        for b in range(2):
+            acc = jnp.zeros((quarter, 128), f32)
+            for a in range(2):
+                at_row = (2 * a + b) * quarter
+                for s in range(2):
+                    acc = acc + jnp.dot(
+                        slots[s][at_row:at_row + quarter],
+                        weights[c, a, s * width:(s + 1) * width, :],
+                        preferred_element_type=f32,
+                    )
+            taps.append(acc)
+        low = taps[0] + pltpu.roll(taps[1], 64, 1)
+        high = pltpu.roll(taps[0], 64, 1) + taps[1]
+        encoded = jnp.where(lane < 64, low[:half_cols], high[half_cols:])
+        hidden_src[c] = jax.nn.gelu(encoded).astype(bf16)
+
+    here = (me_t * n_core + me_s) * n_chan + me_c
+    count = n_tile * n_core * n_chan
+
+    def hidden_copy(i):
+        to = at(*offsets[i])
+        return remote(
+            hidden_src.at[to[1]], hidden_all.at[here + 1],
+            hidden_send.at[i], hidden_recv.at[i], to,
+        )
+
+    for i in range(len(offsets)):
+        hidden_copy(i).start()
+    hidden_all[here + 1] = hidden_src[me_c]
+    hidden_all[0] = jnp.zeros((half_cols, 128), bf16)
+    hidden_all[count + 1] = jnp.zeros((half_cols, 128), bf16)
+    for o in range(1, n_chan):
+        weight_copy(o).wait_send()
+        pass_copy(o).wait_send()
+    for a in range(n_tile):
+        for b in range(n_chan):
+            if a or b:
+                count_copy(a, b).wait_send()
+    for o in turns:
+        for h in range(2):
+            first_copy(h, 0, o, near[h]).wait_send()
+            first_copy(h, 1, o, near[h]).wait_send()
+            second_copy(h, o).wait_send()
+            if o:
+                third_copy(h, o).wait_send()
+    mean_copy.wait_send()
+    for i in range(len(offsets)):
+        hidden_copy(i).wait_recv()
+    line = lax.broadcasted_iota(jnp.int32, (half_cols, 128), 0)
+    for t in range(n_tile):
+        j = jnp.int32(0)
+        for i in range(n_chan):
+            j = jnp.where(owners_ref[t, i] == me_t, i, j)
+        at_piece = (t * n_core + me_s) * n_chan + j + 1
+        total = jnp.zeros((half_cols, 128), f32)
+        for p in range(3):
+            field = hidden_all[at_piece + p - 1].astype(f32)
+            before = jnp.where(line >= 2, pltpu.roll(field, 2, 0), 0.0)
+            after = jnp.where(line < half_cols - 2, pltpu.roll(field, half_cols - 2, 0), 0.0)
+            for q, shifted in enumerate((before, field, after)):
+                total = total + shifted * depth_ref[3 * p + q:3 * p + q + 1, :]
+            if p == 1:
+                middle = field
+        latent = middle + total
+        out_ref[t, 0:half_cols] = latent[:, :64].astype(bf16)
+        out_ref[t, half_cols:] = latent[:, 64:].astype(bf16)
+    for i in range(len(offsets)):
+        hidden_copy(i).wait_send()
+
+
+def fused(observed_values, observed_tile, observed_cell, patch_weight, depth_weight, owners):
+    f32, bf16 = jnp.float32, jnp.bfloat16
+    n_tile, n_chan, n_core = (lax.axis_size(a) for a in ("tile", "chan", "tm"))
+    values = observed_values[0]
+    rows, width = values.shape
+    depth_in, lanes = patch_weight.shape[1:]
+    paired = patch_weight.reshape(2, 2, depth_in, lanes)
+    paired = jnp.concatenate([paired[:, 0], paired[:, 1]], axis=2)
+    depth_rows = depth_weight.astype(f32)
+    depth_rows = jnp.concatenate([depth_rows, depth_rows], axis=1)
+    block = HS * WS // (n_core * n_chan)
+    cells = block // 4
+    dma, vmem = pltpu.SemaphoreType.DMA, pltpu.VMEM
+    whole = pl.BlockSpec(memory_space=pltpu.VMEM)
+    pieces = n_tile * n_core * n_chan
+    out = pl.pallas_call(
+        fused_kernel,
+        out_shape=jax.ShapeDtypeStruct((n_tile, cells, lanes), bf16),
+        in_specs=[whole] * 5 + [pl.BlockSpec(memory_space=pltpu.SMEM)],
+        out_specs=whole,
+        scratch_shapes=[
+            vmem((rows, n_tile * width), bf16),
+            vmem((block, rows), bf16),
+            vmem((1, rows), jnp.int32),
+            vmem((2, 4, n_tile, block, width), bf16),
+            vmem((2, 2, n_tile, block, width), bf16),
+            vmem((2, n_tile, block, width), bf16),
+            vmem((2, n_tile, block, width), bf16),
+            vmem((2, n_tile, block, width), bf16),
+            vmem((2, n_tile, block, width), bf16),
+            vmem((n_tile * n_chan, 8, 128), f32),
+            vmem((n_tile * n_chan, 8, 128), f32),
+            vmem((n_chan, 2, depth_in, 2 * lanes), bf16),
+            vmem((block, width), bf16),
+            vmem((block, width), bf16),
+            vmem((2, block, width), bf16),
+            vmem((n_chan, cells // 2, 128), bf16),
+            vmem((pieces + 2, cells // 2, 128), bf16),
+            dma((3,)), dma((3,)), dma((3,)), dma((3,)),
+            dma((n_tile * n_chan,)), dma((n_tile * n_chan,)),
+            dma((2, 2, n_tile)), dma((2, 2, n_tile)),
+            dma((2, n_tile)), dma((2, n_tile)),
+            dma((2, n_tile)), dma((2, n_tile)),
+            dma, dma,
+            dma((pieces - 1,)), dma((pieces - 1,)),
+        ],
+        compiler_params=pltpu.CompilerParams(
+            collective_id=0, has_side_effects=True, vmem_limit_bytes=48 * 2**20
+        ),
+    )(
+        values, observed_tile.reshape(1, rows), observed_cell, paired, depth_rows, owners
+    )
+    return out.reshape(1, 1, n_tile, cells, lanes)
+
+
+def fits(mesh):
+    tile, chan, tm = (mesh.shape[a] for a in ("tile", "chan", "tm"))
+    return tile == 4 and chan == 4 and tm == 2
+
+
 def solution(mesh):
     placed = (
         P("tm", ("tile", "chan"), None),
@@ -122,7 +460,7 @@
         P(),
     )
     return jax.shard_map(
-        local,
+        fused if fits(mesh) else local,
         mesh=mesh,
         in_specs=placed,
         out_specs=P("tile", "tm", None, None, "chan"),

time: 241 us -> 53.1 us (0.22)
  waiting for transfers between devices: 93.1 us -> 0 us
  Pallas kernels: 0 us -> 48.2 us
  local copies, waits for them, and re-layouts: 45 us -> 3.68 us
  other arithmetic: 27.5 us -> 0.19 us
  matrix products: 24.4 us -> 0 us
  blocking collectives: 21.1 us -> 0 us
  starting transfers between devices: 14.9 us -> 0 us
  between operations: 13.6 us -> 0.05 us
    pallas_call x0 -> x1, Pallas kernels: none -> 48.2 us  [fused(): pl.pallas_call(fused_kernel, out_shape=jax.ShapeDtypeStruct((n_tile, cell...]
    all_to_all x2 -> x0, waiting for transfers between devices: 47.6 us -> none  [the longest x1 47.6 us: local(): lax.all_to_all(sent_values, 'tile', split_axis=0, concat_axis=0, tiled=True)]
    psum x1 -> x0, waiting for transfers between devices: 34.5 us -> none  [local(): lax.psum(totals.astype(jnp.bfloat16), 'chan').astype(jnp.float32)]
    scatter x2 -> x0, local copies, waits for them, and re-layouts: 28.7 us -> none  [the longest x1 16.3 us: pack_rows(): jnp.full((tile_count * capacity,), -1, jnp.int32).at[slot_index].set(placed)]
    dot_general x20 -> x0, matrix products: 24.4 us -> none  [the longest x16 23.7 us: grid_block(): jnp.dot(matches.astype(jnp.bfloat16), arrived_values, preferred_element_t...]
    dynamic_slice x17 -> x0, local copies, waits for them, and re-layouts: 11.7 us -> none  [the longest x16 10.7 us: local(): lax.map(lambda first_cell: grid_block(arrived_values, arrived_cells, firs...]
    all_to_all x2 -> x0, starting transfers between devices: 11.4 us -> none  [the longest x1 6.35 us: local(): lax.all_to_all(sent_cells, 'tile', split_axis=0, concat_axis=0, tiled=True)]
    add x16 -> x0, other arithmetic: 11 us -> none  [grid_block(): cell_ids = first_cell + lax.iota(jnp.int32, 128)]
  transfers between devices with their start and end apart: 6 -> 0, of which waited for: 4 -> 0; matrix products, arithmetic and copies ran while one was open for 6% -> 0% of each run, Pallas kernels for 0% -> 0%
where the time goes in v1:
time: 53.1 us; the launch traced here: 52.1 us
  Pallas kernels  48.2 us (91%)
  local copies, waits for them, and re-layouts  3.68 us (7%)
    pallas_call x1, Pallas kernels, fused(): pl.pallas_call(fused_kernel, out_shape=jax.ShapeDtypeStruct((n_tile, cell...  48.2 us
    unnamed x13, local copies, waits for them, and re-layouts  2.71 us

profile of v1, /device:TPU:0, one launch (start us, length us, event | category | flops | bytes accessed | tf_op | source)
XLA Modules:
  0.0 52.1 jit_solution(9365851163270495522)
XLA Ops:
  0.0 0.0 copy-start
  0.0 1.0 %fusion = (bf16[2,1,256,64]{2,3,1,0:T(8,128)(2,1)S(1)}, bf16[2,1,256,64]{2,3,1,0:T(8,128)(2,1)S(1)}) fusion(bf16[2,2,256,64]{2,3,1,0:T(8,128)(2,1)} %bitcast.11), kind=kLoop, calls=%fused_computation.2 | loop fusion | bytes 262144 | tf_op jit(solution)/shard_map/slice | solution.py:400
  1.0 0.1 copy.9
  1.1 0.0 copy-start.4
  1.1 0.1 copy.10
  1.2 0.0 copy-start.1
  1.2 0.1 pad_maximum_fusion.weight_ref
  1.4 0.4 copy-done.4
  1.8 0.1 maximum_convert_fusion.depth_ref
  1.9 0.0 copy-start.3
  1.9 0.0 copy-done
  1.9 0.1 copy-done.1
  2.0 0.6 %copy-done.3 = s32[4,4]{1,0:T(4,128)S(1)} copy-done((s32[4,4]{1,0:T(4,128)S(1)}, s32[4,4]{1,0:T(4,128)}, u32[]{:S(2)}) %copy-start.3) | copy-done | bytes 88
  2.6 0.0 copy-start.2
  2.6 0.7 %copy-done.2 = s32[1,4096]{1,0:T(1,128)S(1)} copy-done((s32[1,4096]{1,0:T(1,128)S(1)}, s32[1,4096]{1,0:T(1,128)}, u32[]{:S(2)}) %copy-start.2) | copy-done | bytes 16408
  3.3 48.2 %shard_map.64 = bf16[4,64,64]{2,1,0:T(8,128)(2,1)S(1)} custom-call(bf16[4096,128]{1,0:T(8,128)(2,1)S(1)} %bitcast.6, s32[1,4096]{1,0:T(1,128)S(1)} %bitcast.8, s32[1,4096]{1,0:T(1,128)S(1)} %copy-done.2, bf16[2,256,128]{2,1,0:T(8,128)(2,1)S(1)} %pad_maximum_fusion.weight_ref, f32[9,128]{1,0:T(8,128)S(1)} %maximum_convert_fusion.depth_ref, s32[4,4]{1,0:T(4,128)S(1)} %copy-done.3), custom_call_target="tpu_custom_call" | custom-call | tf_op jit(solution)/shard_map/pallas_call | solution.py:408
  51.5 0.6 %copy.12 = bf16[1,1,4,64,64]{4,3,2,1,0:T(8,128)(2,1)} copy(bf16[1,1,4,64,64]{4,3,2,1,0:T(8,128)(2,1)S(1)} %bitcast.7) | data formatting | bytes 65536
Async XLA Ops:
  0.0 1.9 %copy-start = (bf16[1,4096,128]{2,1,0:T(8,128)(2,1)S(1)}, bf16[1,4096,128]{2,1,0:T(8,128)(2,1)}, u32[]{:S(2)}) copy-start(bf16[1,4096,128]{2,1,0:T(8,128)(2,1)} %param.6) | copy-start | bytes 3145732
  1.1 0.7 %copy-start.4 = (bf16[9,64]{1,0:T(8,128)(2,1)S(1)}, bf16[9,64]{1,0:T(8,128)(2,1)}, u32[]{:S(2)}) copy-start(bf16[9,64]{1,0:T(8,128)(2,1)} %param.10) | copy-start | bytes 3460
  1.2 0.7 %copy-start.1 = (s32[1,4096,1]{1,2,0:T(1,128)S(1)}, s32[1,4096,1]{1,2,0:T(1,128)}, u32[]{:S(2)}) copy-start(s32[1,4096,1]{1,2,0:T(1,128)} %param.7) | copy-start | bytes 49156
  1.9 0.7 %copy-start.3 = (s32[4,4]{1,0:T(4,128)S(1)}, s32[4,4]{1,0:T(4,128)}, u32[]{:S(2)}) copy-start(s32[4,4]{1,0:T(4,128)} %owners_ref.1) | copy-start | bytes 196
  2.6 0.7 %copy-start.2 = (s32[1,4096]{1,0:T(1,128)S(1)}, s32[1,4096]{1,0:T(1,128)}, u32[]{:S(2)}) copy-start(s32[1,4096]{1,0:T(1,128)} %cell_ref.1) | copy-start | bytes 49156

commit v2 on v1

--- a/solution.py
+++ b/solution.py
@@ -116,9 +116,11 @@
 
 
 def fused_kernel(
-    values_ref, tile_ref, cell_ref, weight_ref, depth_ref, owners_ref, out_ref,
+    values_hbm, column_hbm, tile_hbm, cell_hbm, weight_hbm, depth_hbm, owners_hbm, out_ref,
+    values_ref, column_ref, tile_ref, cell_ref, depth_ref, owners_ref,
     masked, onehot, position, partial, first, second_src, second, third_src, third,
     count_src, count_in, weights, mean_src, mean_in, means, hidden_src, hidden_all,
+    load_sems,
     weight_send, weight_recv, pass_send, pass_recv, count_send, count_recv,
     first_send, first_recv, second_send, second_recv, third_send, third_recv,
     mean_send, mean_recv, hidden_send, hidden_recv,
@@ -129,12 +131,14 @@
     rows, width = values_ref.shape
     block = partial.shape[3]
     quarter = block // 4
+    half_cols = WS // 2
     flip_x = me_c + 1 - 2 * (me_c % 2)
     flip_y = (me_c + 2) % 4
     diagonal = 3 - me_c
     near = (flip_x, flip_y)
     far = (flip_y, flip_x)
     other = 1 - me_s
+    last = n_tile - 1
 
     def remote(source, target, send, recv, device):
         return pltpu.make_async_remote_copy(
@@ -149,40 +153,142 @@
     def at(a, b, c):
         return ((me_t + a) % n_tile, (me_c + b) % n_chan, (me_s + c) % n_core)
 
+    loads = [
+        pltpu.make_async_copy(source, target, load_sems.at[i])
+        for i, (source, target) in enumerate((
+            (weight_hbm, weights.at[me_c]), (column_hbm, column_ref), (cell_hbm, cell_ref),
+            (values_hbm, values_ref), (tile_hbm, tile_ref), (depth_hbm, depth_ref),
+            (owners_hbm, owners_ref),
+        ))
+    ]
+    for load in loads:
+        load.start()
     barrier = pltpu.get_barrier_semaphore()
     for offset in offsets:
         pl.semaphore_signal(
             barrier, inc=1, device_id=at(*offset), device_id_type=pl.DeviceIdType.MESH
         )
 
+    def weight_copy(o):
+        here = weights.at[me_c, me_s]
+        return remote(
+            here, here, weight_send.at[o - 1], weight_recv.at[o - 1],
+            (me_t, (me_c + o) % n_chan, me_s),
+        )
+
+    def pass_copy(o):
+        here = weights.at[(me_c - o + n_chan) % n_chan, me_s]
+        return remote(
+            here, here, pass_send.at[o - 1], pass_recv.at[o - 1], (me_t, me_c, other)
+        )
+
+    def count_copy(a, b):
+        i = a * n_chan + b
+        to = ((me_t + a) % n_tile, (me_c + b) % n_chan, me_s)
+        return remote(
+            count_src.at[to[0] * n_chan + to[1]], count_in.at[i],
+            count_send.at[i], count_recv.at[i], to,
+        )
+
+    def first_copy(h, k, m, to):
+        return remote(
+            partial.at[h, k, m], first.at[h, k, m],
+            first_send.at[h, k, m], first_recv.at[h, k, m], (me_t, to, me_s),
+        )
+
+    def second_copy(h, m):
+        return remote(
+            second_src.at[h, m], second.at[h, m],
+            second_send.at[h, m], second_recv.at[h, m], (me_t, far[h], me_s),
+        )
+
+    def third_copy(h, m):
+        return remote(
+            third_src.at[h, m], third.at[h, m],
+            third_send.at[h, m], third_recv.at[h, m],
+            ((me_t + m + 1) % n_tile, me_c, me_s),
+        )
+
+    loads[1].wait()
+    loads[2].wait()
     cell = cell_ref[...]
     row, col = cell // WS, cell % WS
-    half_cols = WS // 2
-    band = row // 4
     position[...] = (
-        band * block + (row % 2) * (2 * quarter) + (col % 2) * quarter
+        (row // 4) * block + (row % 2) * (2 * quarter) + (col % 2) * quarter
         + ((row % 4) // 2) * half_cols + col // 2
     )
-    weights[me_c] = weight_ref[...]
-
-    def mask_rows(i, carry):
-        span = pl.ds(pl.multiple_of(i * 128, 128), 128)
-        tiles = jnp.broadcast_to(tile_ref[:, span].astype(f32), (128, 128))
-        tiles = jnp.transpose(tiles)
-        taken = values_ref[span, :].astype(f32)
-        for t in range(n_tile):
-            masked[span, t * width:(t + 1) * width] = jnp.where(
-                tiles == float(t), taken, 0.0
+    columns = jnp.transpose(column_ref[...].astype(f32))
+    loads[0].wait()
+    loads[3].wait()
+    for i in range(rows // 128):
+        tiles = jnp.broadcast_to(columns[:, i:i + 1], (128, width))
+        taken = values_ref[i * 128:(i + 1) * 128, :].astype(f32)
+        for m in range(n_tile):
+            wanted = ((me_t + m + 1) % n_tile).astype(f32)
+            masked[i * 128:(i + 1) * 128, m * width:(m + 1) * width] = jnp.where(
+                tiles == wanted, taken, 0.0
             ).astype(bf16)
+    pl.semaphore_wait(barrier, len(offsets))
+    for o in range(1, n_chan):
+        weight_copy(o).start()
+
+    def grid_block(half, step, carry):
+        h, k = step % 2, step // 2
+        to = near[0] * (1 - h) + near[1] * h
+        away = near[1] * (1 - h) + near[0] * h
+        if half == 0:
+            picks = (diagonal, to, away, me_c)
+            j = sum(jnp.where(k == i, p, 0) for i, p in enumerate(picks))
+            base = (h * n_chan + j) * block
+            ids = lax.broadcasted_iota(jnp.int32, (block, rows), 0)
+            onehot[step] = (ids == position[...] - base).astype(bf16)
+        low = half * 2 * width
+        sums = jnp.dot(
+            onehot[step], masked[:, low:low + 2 * width], preferred_element_type=f32
+        )
+        for u in range(2):
+            partial[h, k, 2 * half + u] = sums[:, u * width:(u + 1) * width].astype(bf16)
+
+        @pl.when(k < 2)
+        def _():
+            for u in range(2):
+                first_copy(h, k, 2 * half + u, to).start()
+
         return carry
 
-    lax.fori_loop(0, rows // 128, mask_rows, 0)
-
+    def do_second(half):
+        for m in (2 * half, 2 * half + 1):
+            for h in range(2):
+                first_copy(h, 0, m, near[h]).wait_recv()
+                second_src[h, m] = (
+                    partial[h, 2, m].astype(f32) + first[h, 0, m].astype(f32)
+                ).astype(bf16)
+                second_copy(h, m).start()
+
+    def do_third(half):
+        for m in (2 * half, 2 * half + 1):
+            for h in range(2):
+                first_copy(h, 1, m, near[h]).wait_recv()
+                second_copy(h, m).wait_recv()
+                third_src[h, m] = (
+                    partial[h, 3, m].astype(f32)
+                    + first[h, 1, m].astype(f32)
+                    + second[h, m].astype(f32)
+                ).astype(bf16)
+                if m != last:
+                    third_copy(h, m).start()
+
+    lax.fori_loop(0, 8, functools.partial(grid_block, 0), 0)
+    do_second(0)
+    lax.fori_loop(0, 8, functools.partial(grid_block, 1), 0)
+    do_third(0)
+    do_second(1)
+
+    loads[4].wait()
     pos = position[...]
     inner = pos % block
-    half = pos // (block * n_chan)
-    piece = (pos // block) % n_chan
-    code = ((tile_ref[...] * n_chan + piece) * 8 + half * 2 + inner // 128)
+    code = (tile_ref[...] * n_chan + (pos // block) % n_chan) * 8
+    code = code + (pos // (block * n_chan)) * 2 + inner // 128
     code_ids = lax.broadcasted_iota(jnp.int32, (n_tile * n_chan * 8, rows), 0)
     lane_ids = lax.broadcasted_iota(jnp.int32, (128, rows), 0)
     counts = lax.dot_general(
@@ -190,104 +296,23 @@
         (((1,), (1,)), ((), ())), preferred_element_type=f32,
     )
     count_src[...] = counts.reshape(n_tile * n_chan, 8, 128)
-
-    pl.semaphore_wait(barrier, len(offsets))
-
-    def weight_copy(o):
-        here = weights.at[me_c, me_s]
-        return remote(
-            here, here, weight_send.at[o - 1], weight_recv.at[o - 1],
-            (me_t, (me_c + o) % n_chan, me_s),
-        )
-
-    def pass_copy(o):
-        here = weights.at[(me_c - o + n_chan) % n_chan, me_s]
-        return remote(
-            here, here, pass_send.at[o - 1], pass_recv.at[o - 1], (me_t, me_c, other)
-        )
-
-    def count_copy(a, b):
-        i = a * n_chan + b
-        to = ((me_t + a) % n_tile, (me_c + b) % n_chan, me_s)
-        return remote(
-            count_src.at[to[0] * n_chan + to[1]], count_in.at[i],
-            count_send.at[i], count_recv.at[i], to,
-        )
-
-    def first_copy(h, k, o, to):
-        t = (me_t + o) % n_tile
-        return remote(
-            partial.at[h, k, t], first.at[h, k, t],
-            first_send.at[h, k, o], first_recv.at[h, k, o], (me_t, to, me_s),
-        )
-
-    def second_copy(h, o):
-        t = (me_t + o) % n_tile
-        return remote(
-            second_src.at[h, t], second.at[h, t],
-            second_send.at[h, o], second_recv.at[h, o], (me_t, far[h], me_s),
-        )
-
-    def third_copy(h, o):
-        t = (me_t + o) % n_tile
-        return remote(
-            third_src.at[h, o], third.at[h, o],
-            third_send.at[h, o], third_recv.at[h, o], (t, me_c, me_s),
-        )
-
-    turns = tuple(range(1, n_tile)) + (0,)
-    for o in range(1, n_chan):
-        weight_copy(o).start()
     for a in range(n_tile):
         for b in range(n_chan):
             if a or b:
                 count_copy(a, b).start()
-
-    def grid_block(step, carry):
-        h, k = step % 2, step // 2
-        to = near[0] * (1 - h) + near[1] * h
-        away = near[1] * (1 - h) + near[0] * h
-        picks = (diagonal, to, away, me_c)
-        j = sum(p * (1 - jnp.minimum(jnp.abs(k - i), 1)) for i, p in enumerate(picks))
-        base = (h * n_chan + j) * block
-        ids = lax.broadcasted_iota(jnp.int32, (block, rows), 0)
-        onehot[...] = (ids == position[...] - base).astype(bf16)
-        sums = jnp.dot(onehot[...], masked[...], preferred_element_type=f32)
-        for t in range(n_tile):
-            partial[h, k, t] = sums[:, t * width:(t + 1) * width].astype(bf16)
-
-        @pl.when(k < 2)
-        def _():
-            for o in turns:
-                first_copy(h, k, o, to).start()
-
-        return carry
-
-    lax.fori_loop(0, 8, grid_block, 0)
-
-    for o in turns:
-        t = (me_t + o) % n_tile
-        for h in range(2):
-            first_copy(h, 0, o, near[h]).wait_recv()
-            second_src[h, t] = (
-                partial[h, 2, t].astype(f32) + first[h, 0, t].astype(f32)
-            ).astype(bf16)
-            second_copy(h, o).start()
     for o in range(1, n_chan):
         weight_copy(o).wait_recv()
         pass_copy(o).start()
-    for o in turns:
-        t = (me_t + o) % n_tile
-        for h in range(2):
-            first_copy(h, 1, o, near[h]).wait_recv()
-            second_copy(h, o).wait_recv()
-            third_src[h, o] = (
-                partial[h, 3, t].astype(f32)
-                + first[h, 1, t].astype(f32)
-                + second[h, t].astype(f32)
-            ).astype(bf16)
-            if o:
-                third_copy(h, o).start()
+    do_third(1)
+
+    here = (me_t * n_core + me_s) * n_chan + me_c
+    count = n_tile * n_core * n_chan
+    hidden_all[0] = jnp.zeros((half_cols, 128), bf16)
+    hidden_all[count + 1] = jnp.zeros((half_cols, 128), bf16)
+    loads[5].wait()
+    loads[6].wait()
+    taps9 = depth_ref[...].astype(f32)
+    taps9 = jnp.concatenate([taps9, taps9], axis=1)
 
     total = count_src[me_t * n_chan + me_c]
     for a in range(n_tile):
@@ -298,11 +323,11 @@
     divisor = jnp.maximum(total, 1.0)
 
     for h in range(2):
-        for o in range(1, n_tile):
-            third_copy(h, o).wait_recv()
-        summed = third_src[h, 0].astype(f32)
-        for o in range(1, n_tile):
-            summed = summed + third[h, o].astype(f32)
+        for m in range(last):
+            third_copy(h, m).wait_recv()
+        summed = third_src[h, last].astype(f32)
+        for m in range(last):
+            summed = summed + third[h, m].astype(f32)
         for u in range(block // 128):
             line = divisor[h * 2 + u:h * 2 + u + 1, :]
             each = jnp.transpose(jnp.broadcast_to(line, (128, 128)))
@@ -318,17 +343,19 @@
     even = me_s == 0
     slots = (jnp.where(even, mine, theirs), jnp.where(even, theirs, mine))
     lane = lax.broadcasted_iota(jnp.int32, (half_cols, 128), 1)
+    lanes = weights.shape[3]
     for c in range(n_chan):
         taps = []
         for b in range(2):
-            acc = jnp.zeros((quarter, 128), f32)
+            acc = jnp.zeros((quarter, 2 * lanes), f32)
             for a in range(2):
                 at_row = (2 * a + b) * quarter
+                kernel = weights[c, a].reshape(2 * lanes, 2 * width)
                 for s in range(2):
-                    acc = acc + jnp.dot(
+                    acc = acc + lax.dot_general(
                         slots[s][at_row:at_row + quarter],
-                        weights[c, a, s * width:(s + 1) * width, :],
-                        preferred_element_type=f32,
+                        kernel[:, s * width:(s + 1) * width],
+                        (((1,), (1,)), ((), ())), preferred_element_type=f32,
                     )
             taps.append(acc)
         low = taps[0] + pltpu.roll(taps[1], 64, 1)
@@ -336,9 +363,6 @@
         encoded = jnp.where(lane < 64, low[:half_cols], high[half_cols:])
         hidden_src[c] = jax.nn.gelu(encoded).astype(bf16)
 
-    here = (me_t * n_core + me_s) * n_chan + me_c
-    count = n_tile * n_core * n_chan
-
     def hidden_copy(i):
         to = at(*offsets[i])
         return remote(
@@ -346,11 +370,18 @@
             hidden_send.at[i], hidden_recv.at[i], to,
         )
 
-    for i in range(len(offsets)):
-        hidden_copy(i).start()
+    def each_hidden(column, act):
+        for i, (_, b, c) in enumerate(offsets):
+            if c == 0:
+                act(hidden_copy(i))
+        for i, (_, b, c) in enumerate(offsets):
+            if c:
+                @pl.when(column(b) % (n_chan - 1) == 0)
+                def _():
+                    act(hidden_copy(i))
+
+    each_hidden(lambda b: me_c, lambda copy: copy.start())
     hidden_all[here + 1] = hidden_src[me_c]
-    hidden_all[0] = jnp.zeros((half_cols, 128), bf16)
-    hidden_all[count + 1] = jnp.zeros((half_cols, 128), bf16)
     for o in range(1, n_chan):
         weight_copy(o).wait_send()
         pass_copy(o).wait_send()
@@ -358,16 +389,15 @@
         for b in range(n_chan):
             if a or b:
                 count_copy(a, b).wait_send()
-    for o in turns:
+    for m in range(n_tile):
         for h in range(2):
-            first_copy(h, 0, o, near[h]).wait_send()
-            first_copy(h, 1, o, near[h]).wait_send()
-            second_copy(h, o).wait_send()
-            if o:
-                third_copy(h, o).wait_send()
+            first_copy(h, 0, m, near[h]).wait_send()
+            first_copy(h, 1, m, near[h]).wait_send()
+            second_copy(h, m).wait_send()
+            if m != last:
+                third_copy(h, m).wait_send()
     mean_copy.wait_send()
-    for i in range(len(offsets)):
-        hidden_copy(i).wait_recv()
+    each_hidden(lambda b: (me_c + n_chan - b) % n_chan, lambda copy: copy.wait_recv())
     line = lax.broadcasted_iota(jnp.int32, (half_cols, 128), 0)
     for t in range(n_tile):
         j = jnp.int32(0)
@@ -380,40 +410,41 @@
             before = jnp.where(line >= 2, pltpu.roll(field, 2, 0), 0.0)
             after = jnp.where(line < half_cols - 2, pltpu.roll(field, half_cols - 2, 0), 0.0)
             for q, shifted in enumerate((before, field, after)):
-                total = total + shifted * depth_ref[3 * p + q:3 * p + q + 1, :]
+                total = total + shifted * taps9[3 * p + q:3 * p + q + 1, :]
             if p == 1:
                 middle = field
         latent = middle + total
         out_ref[t, 0:half_cols] = latent[:, :64].astype(bf16)
         out_ref[t, half_cols:] = latent[:, 64:].astype(bf16)
-    for i in range(len(offsets)):
-        hidden_copy(i).wait_send()
+    each_hidden(lambda b: me_c, lambda copy: copy.wait_send())
 
 
 def fused(observed_values, observed_tile, observed_cell, patch_weight, depth_weight, owners):
-    f32, bf16 = jnp.float32, jnp.bfloat16
+    f32, bf16, i32 = jnp.float32, jnp.bfloat16, jnp.int32
     n_tile, n_chan, n_core = (lax.axis_size(a) for a in ("tile", "chan", "tm"))
     values = observed_values[0]
     rows, width = values.shape
     depth_in, lanes = patch_weight.shape[1:]
-    paired = patch_weight.reshape(2, 2, depth_in, lanes)
-    paired = jnp.concatenate([paired[:, 0], paired[:, 1]], axis=2)
-    depth_rows = depth_weight.astype(f32)
-    depth_rows = jnp.concatenate([depth_rows, depth_rows], axis=1)
+    turned = jnp.swapaxes(patch_weight, 1, 2).reshape(2, 2, lanes, depth_in)
     block = HS * WS // (n_core * n_chan)
     cells = block // 4
     dma, vmem = pltpu.SemaphoreType.DMA, pltpu.VMEM
-    whole = pl.BlockSpec(memory_space=pltpu.VMEM)
     pieces = n_tile * n_core * n_chan
     out = pl.pallas_call(
         fused_kernel,
         out_shape=jax.ShapeDtypeStruct((n_tile, cells, lanes), bf16),
-        in_specs=[whole] * 5 + [pl.BlockSpec(memory_space=pltpu.SMEM)],
-        out_specs=whole,
+        in_specs=[pl.BlockSpec(memory_space=pl.ANY)] * 7,
+        out_specs=pl.BlockSpec(memory_space=pltpu.VMEM),
         scratch_shapes=[
+            vmem((rows, width), bf16),
+            vmem((rows // 128, 128), i32),
+            vmem((1, rows), i32),
+            vmem((1, rows), i32),
+            vmem(depth_weight.shape, bf16),
+            pltpu.SMEM(owners.shape, i32),
             vmem((rows, n_tile * width), bf16),
-            vmem((block, rows), bf16),
-            vmem((1, rows), jnp.int32),
+            vmem((8, block, rows), bf16),
+            vmem((1, rows), i32),
             vmem((2, 4, n_tile, block, width), bf16),
             vmem((2, 2, n_tile, block, width), bf16),
             vmem((2, n_tile, block, width), bf16),
@@ -422,12 +453,13 @@
             vmem((2, n_tile, block, width), bf16),
             vmem((n_tile * n_chan, 8, 128), f32),
             vmem((n_tile * n_chan, 8, 128), f32),
-            vmem((n_chan, 2, depth_in, 2 * lanes), bf16),
+            vmem((n_chan, 2, 2, lanes, depth_in), bf16),
             vmem((block, width), bf16),
             vmem((block, width), bf16),
             vmem((2, block, width), bf16),
             vmem((n_chan, cells // 2, 128), bf16),
             vmem((pieces + 2, cells // 2, 128), bf16),
+            dma((7,)),
             dma((3,)), dma((3,)), dma((3,)), dma((3,)),
             dma((n_tile * n_chan,)), dma((n_tile * n_chan,)),
             dma((2, 2, n_tile)), dma((2, 2, n_tile)),
@@ -437,10 +469,11 @@
             dma((pieces - 1,)), dma((pieces - 1,)),
         ],
         compiler_params=pltpu.CompilerParams(
-            collective_id=0, has_side_effects=True, vmem_limit_bytes=48 * 2**20
+            collective_id=0, has_side_effects=True, vmem_limit_bytes=56 * 2**20
         ),
     )(
-        values, observed_tile.reshape(1, rows), observed_cell, paired, depth_rows, owners
+        values, observed_tile.reshape(rows // 128, 128), observed_tile.reshape(1, rows),
+        observed_cell, turned, depth_weight, owners,
     )
     return out.reshape(1, 1, n_tile, cells, lanes)
 

time: 53.1 us -> 50.6 us (0.953); the launches traced: 52.1 us -> 50.4 us
  local copies, waits for them, and re-layouts: 3.68 us -> 1.47 us
  Pallas kernels: 48.2 us -> 48.9 us
    unnamed x13 -> x1, local copies, waits for them, and re-layouts: 2.71 us -> 1.47 us
    slice x1 -> x0, local copies, waits for them, and re-layouts: 0.97 us -> none  [fused(): paired = jnp.concatenate([paired[:, 0], paired[:, 1]], axis=2)]
    pallas_call x1, Pallas kernels: 48.2 us -> 48.9 us  [fused(): pl.pallas_call(fused_kernel, out_shape=jax.ShapeDtypeStruct((n_tile, cell...]
where the time goes in v2:
time: 50.6 us; the launch traced here: 50.4 us
  Pallas kernels  48.9 us (97%)
  local copies, waits for them, and re-layouts  1.47 us (3%)
    pallas_call x1, Pallas kernels, fused(): pl.pallas_call(fused_kernel, out_shape=jax.ShapeDtypeStruct((n_tile, cell...  48.9 us
    unnamed x1, local copies, waits for them, and re-layouts  1.47 us

profile of v2, /device:TPU:0, one launch (start us, length us, event | category | flops | bytes accessed | tf_op | source)
XLA Modules:
  0.0 50.4 jit_solution(9564895866433733210)
XLA Ops:
  0.0 48.9 %shard_map.64 = bf16[4,64,64]{2,1,0:T(8,128)(2,1)} custom-call(bf16[4096,128]{1,0:T(8,128)(2,1)} %bitcast.7, s32[32,128]{1,0:T(8,128)} %bitcast.10, s32[1,4096]{1,0:T(1,128)} %bitcast.11, s32[1,4096]{1,0:T(1,128)} %cell_hbm.1, bf16[2,2,64,256]{3,2,1,0:T(8,128)(2,1)} %bitcast.9, bf16[9,64]{1,0:T(8,128)(2,1)} %depth_hbm.1, s32[4,4]{1,0:T(4,128)} %owners_hbm.1), custom_call_target="tpu_custom_call" | custom-call | tf_op jit(solution)/shard_map/pallas_call | solution.py:433
  48.9 1.5 %copy.8 = bf16[1,1,4,64,64]{4,3,2,1,0:T(8,128)(2,1)} copy(bf16[1,1,4,64,64]{4,3,2,1,0:T(8,128)(2,1)} %bitcast.8) | data formatting | bytes 65536

commit v3 on v2

--- a/solution.py
+++ b/solution.py
@@ -228,33 +228,27 @@
             masked[i * 128:(i + 1) * 128, m * width:(m + 1) * width] = jnp.where(
                 tiles == wanted, taken, 0.0
             ).astype(bf16)
-    pl.semaphore_wait(barrier, len(offsets))
-    for o in range(1, n_chan):
-        weight_copy(o).start()
-
-    def grid_block(half, step, carry):
-        h, k = step % 2, step // 2
-        to = near[0] * (1 - h) + near[1] * h
-        away = near[1] * (1 - h) + near[0] * h
-        if half == 0:
-            picks = (diagonal, to, away, me_c)
+    ids = lax.broadcasted_iota(jnp.int32, (block, rows), 0)
+
+    def grid_block(k, carry):
+        for h in range(2):
+            picks = (diagonal, near[h], far[h], me_c)
             j = sum(jnp.where(k == i, p, 0) for i, p in enumerate(picks))
             base = (h * n_chan + j) * block
-            ids = lax.broadcasted_iota(jnp.int32, (block, rows), 0)
-            onehot[step] = (ids == position[...] - base).astype(bf16)
-        low = half * 2 * width
-        sums = jnp.dot(
-            onehot[step], masked[:, low:low + 2 * width], preferred_element_type=f32
-        )
-        for u in range(2):
-            partial[h, k, 2 * half + u] = sums[:, u * width:(u + 1) * width].astype(bf16)
-
-        @pl.when(k < 2)
-        def _():
-            for u in range(2):
-                first_copy(h, k, 2 * half + u, to).start()
-
+            onehot[h * block:(h + 1) * block] = (ids == position[...] - base).astype(bf16)
+        sums = jnp.dot(onehot[...], masked[...], preferred_element_type=f32)
+        for h in range(2):
+            for m in range(n_tile):
+                partial[h, k, m] = sums[
+                    h * block:(h + 1) * block, m * width:(m + 1) * width
+                ].astype(bf16)
         return carry
+
+    def do_first(half):
+        for k in range(2):
+            for m in (2 * half, 2 * half + 1):
+                for h in range(2):
+                    first_copy(h, k, m, near[h]).start()
 
     def do_second(half):
         for m in (2 * half, 2 * half + 1):
@@ -278,12 +272,17 @@
                 if m != last:
                     third_copy(h, m).start()
 
-    lax.fori_loop(0, 8, functools.partial(grid_block, 0), 0)
+    lax.fori_loop(0, 2, grid_block, 0)
+    pl.semaphore_wait(barrier, len(offsets))
+    do_first(0)
+    lax.fori_loop(2, 3, grid_block, 0)
     do_second(0)
-    lax.fori_loop(0, 8, functools.partial(grid_block, 1), 0)
+    do_first(1)
+    lax.fori_loop(3, 4, grid_block, 0)
     do_third(0)
     do_second(1)
-
+    for o in range(1, n_chan):
+        weight_copy(o).start()
     loads[4].wait()
     pos = position[...]
     inner = pos % block
@@ -300,9 +299,6 @@
         for b in range(n_chan):
             if a or b:
                 count_copy(a, b).start()
-    for o in range(1, n_chan):
-        weight_copy(o).wait_recv()
-        pass_copy(o).start()
     do_third(1)
 
     here = (me_t * n_core + me_s) * n_chan + me_c
@@ -322,6 +318,9 @@
                 total = total + count_in[a * n_chan + b]
     divisor = jnp.maximum(total, 1.0)
 
+    for o in range(1, n_chan):
+        weight_copy(o).wait_recv()
+        pass_copy(o).start()
     for h in range(2):
         for m in range(last):
             third_copy(h, m).wait_recv()
@@ -374,8 +373,7 @@
         for i, (_, b, c) in enumerate(offsets):
             if c == 0:
                 act(hidden_copy(i))
-        for i, (_, b, c) in enumerate(offsets):
-            if c:
+            else:
                 @pl.when(column(b) % (n_chan - 1) == 0)
                 def _():
                     act(hidden_copy(i))
@@ -443,7 +441,7 @@
             vmem(depth_weight.shape, bf16),
             pltpu.SMEM(owners.shape, i32),
             vmem((rows, n_tile * width), bf16),
-            vmem((8, block, rows), bf16),
+            vmem((2 * block, rows), bf16),
             vmem((1, rows), i32),
             vmem((2, 4, n_tile, block, width), bf16),
             vmem((2, 2, n_tile, block, width), bf16),

time: 50.6 us -> 45.8 us (0.905)
  Pallas kernels: 48.9 us -> 44.2 us
    pallas_call x1, Pallas kernels: 48.9 us -> 44.2 us  [fused(): pl.pallas_call(fused_kernel, out_shape=jax.ShapeDtypeStruct((n_tile, cell...]
where the time goes in v3:
time: 45.8 us; the launch traced here: 45.7 us
  Pallas kernels  44.2 us (97%)
  local copies, waits for them, and re-layouts  1.47 us (3%)
    pallas_call x1, Pallas kernels, fused(): pl.pallas_call(fused_kernel, out_shape=jax.ShapeDtypeStruct((n_tile, cell...  44.2 us
    unnamed x1, local copies, waits for them, and re-layouts  1.47 us

profile of v3, /device:TPU:0, one launch (start us, length us, event | category | flops | bytes accessed | tf_op | source)
XLA Modules:
  0.0 45.7 jit_solution(1989625704746201410)
XLA Ops:
  0.0 44.2 %shard_map.64 = bf16[4,64,64]{2,1,0:T(8,128)(2,1)} custom-call(bf16[4096,128]{1,0:T(8,128)(2,1)} %bitcast.7, s32[32,128]{1,0:T(8,128)} %bitcast.10, s32[1,4096]{1,0:T(1,128)} %bitcast.11, s32[1,4096]{1,0:T(1,128)} %cell_hbm.1, bf16[2,2,64,256]{3,2,1,0:T(8,128)(2,1)} %bitcast.9, bf16[9,64]{1,0:T(8,128)(2,1)} %depth_hbm.1, s32[4,4]{1,0:T(4,128)} %owners_hbm.1), custom_call_target="tpu_custom_call" | custom-call | tf_op jit(solution)/shard_map/pallas_call | solution.py:431
  44.2 1.5 %copy.8 = bf16[1,1,4,64,64]{4,3,2,1,0:T(8,128)(2,1)} copy(bf16[1,1,4,64,64]{4,3,2,1,0:T(8,128)(2,1)} %bitcast.8) | data formatting | bytes 65536
